TPU v7x, 32 devices: a whole 2x2x4 slice. The times are simulated.
32 devices in a mesh: tower: 2 (over core), depth: 4 (over z), sub: 4 (over y, x).
Axes of the slice: x: 2, y: 2, z: 4, core: 2. Of those that a mesh axis runs over, the one named last changes fastest.
Arguments:
- embeds: bfloat16 [2, 16384, 1024], P('tower', ('depth', 'sub')), may hold values from -700 to 700
- counts: int32 [16], P(('depth', 'sub')), may hold values from 256 to 1024, as said below
Outputs:
- row_grads: bfloat16 [2, 16384, 1024], P('tower', ('depth', 'sub'))
- corr_mean: float32 [], replicated
Inputs may be any that keep to these rules, and one draw needn't show every extreme that they name: `counts`: block b holds at least 256 and at most 256 + 768 * b // 15 valid samples; the first block holds exactly 256 and the last block is full.
All inputs are finite; a program needn't handle non-finite values.
Results may differ from a plain program's by a relative error of at most 0.022.
Values may be sent and summed in bfloat16 or wider, within the bound.
No kernel may reach another device: no remote copies, remote signals or barrier semaphores. Data moves between devices by JAX's collectives and lax.ppermute only.
A program may use at most 128 MiB of HBM per device.

v0:
```python
import jax
import jax.numpy as jnp
from jax import lax
from jax.sharding import PartitionSpec as P

REG = 0.001
contract_rows = (((0,), (0,)), ((), ()))


def from_partner(value, axis, apart):
    mask = 2**apart
    pairs = [(source, source ^ mask) for source in range(lax.axis_size(axis))]
    return lax.ppermute(value, axis, pairs)


def whitening(block_rows, valid_rows, gram_total, column_sum, count_total):
    feature_width = block_rows.shape[1]
    column_mean = column_sum / count_total
    covariance = (gram_total - jnp.outer(column_sum, column_mean)) / (
        count_total - 1.0
    ) + REG * jnp.eye(feature_width, dtype=jnp.float32)
    factor_lower = jnp.linalg.cholesky(covariance)
    centered = jnp.where(
        valid_rows[:, None], block_rows.astype(jnp.float32) - column_mean[None, :], 0.0
    )
    whitened = jax.scipy.linalg.solve_triangular(factor_lower, centered.T, lower=True).T
    return (whitened.astype(jnp.bfloat16), factor_lower)


def gradient_rows(own_white, other_white, turned, factor_lower, valid_rows):
    product_rows = jnp.dot(own_white, turned, preferred_element_type=jnp.float32)
    residual = (other_white.astype(jnp.float32) - product_rows).astype(jnp.bfloat16)
    back_rows = lax.dot_general(
        residual, turned, (((1,), (1,)), ((), ())), preferred_element_type=jnp.float32
    )
    solved = jax.scipy.linalg.solve_triangular(factor_lower, back_rows.T, lower=True, trans=1).T
    return jnp.where(valid_rows[:, None], solved, 0.0).astype(jnp.bfloat16)


def on_device(embeds, counts):
    block_rows = embeds[0]
    rows_local = block_rows.shape[0]
    feature_width = block_rows.shape[1]
    valid_rows = lax.iota(jnp.int32, rows_local) < counts[0]
    log_tower = lax.axis_index("tower") == 0
    count_part = counts.astype(jnp.float32)
    masked = jnp.where(valid_rows[:, None], block_rows, jnp.zeros_like(block_rows))
    gram_part = lax.dot_general(masked, masked, contract_rows, preferred_element_type=jnp.float32)
    column_part = jnp.sum(masked, axis=0, dtype=jnp.float32)
    gram_total, column_sum, count_sums = lax.psum(
        (gram_part, column_part, count_part), ("depth", "sub")
    )
    count_total = count_sums[0]
    whitened, factor_lower = whitening(block_rows, valid_rows, gram_total, column_sum, count_total)
    partner_rows = from_partner(whitened, "tower", 0)
    log_white = jnp.where(log_tower, whitened, partner_rows)
    image_white = jnp.where(log_tower, partner_rows, whitened)
    half_rows = rows_local // 2
    first_row = lax.axis_index("tower") * half_rows
    log_part = lax.dynamic_slice_in_dim(log_white, first_row, half_rows, 0)
    image_part = lax.dynamic_slice_in_dim(image_white, first_row, half_rows, 0)
    group_size = lax.axis_size(("tower", "depth", "sub"))
    cross_part = lax.dot_general(
        log_part, image_part, contract_rows, preferred_element_type=jnp.float32
    )
    cross_share = lax.psum_scatter(
        cross_part.reshape(group_size, -1),
        ("tower", "depth", "sub"),
        scatter_dimension=0,
        tiled=True,
    )
    share_bf = (cross_share / (count_total - 1.0)).astype(jnp.bfloat16)
    gathered = lax.all_gather(share_bf, ("tower", "depth", "sub"), axis=0, tiled=True)
    cross_bf = gathered.reshape(feature_width, feature_width)
    corr_mean = jnp.sum(jnp.square(cross_bf.astype(jnp.float32))) / feature_width
    turned = jnp.where(log_tower, cross_bf, cross_bf.T)
    gradient = gradient_rows(whitened, partner_rows, turned, factor_lower, valid_rows)
    return (gradient[None], corr_mean)


def solution(mesh):
    placed = (P("tower", ("depth", "sub"), None), P(("depth", "sub")))
    return jax.shard_map(
        on_device,
        mesh=mesh,
        in_specs=placed,
        out_specs=(P("tower", ("depth", "sub"), None), P()),
        check_vma=False,
    )
```

profile of v0, /device:TPU:0, one launch (start us, length us, event | category | flops | bytes accessed | tf_op | source)
XLA Modules:
  0.0 871.4 jit_solution(1099078158956488727)
XLA Ops:
  7.9 6.7 fusion.19
  14.6 2.9 copy.61
  18.0 47.7 %all-reduce.2 = (f32[1024]{0:T(1024)S(1)}, f32[]{:T(128)}) all-reduce(f32[1024]{0:T(1024)S(1)} %convert_reduce_fusion, f32[]{:T(128)} %bitcast.3), channel_id=1, replica_groups=mesh['tower'=2,'depth'=4,'sub'=4] {'depth','sub'}, use_global_device_ids=true, to_apply=%region_2.3 | all-reduce | flops 1025 | bytes 8200 | tf_op jit(solution)/shard_map/psum | solution.py:50
  67.0 120.0 %all-reduce.6.cloned.1.call-done = f32[1024,1024]{0,1:T(8,128)} async-done(((f32[1024,1024]{0,1:T(8,128)}), f32[1024,1024]{0,1:T(8,128)}) %all-reduce.6.cloned.1.call-update) | async-done | bytes 4194320 | tf_op jit(solution)/shard_map/psum | solution.py:50
  187.0 5.7 select_add_fusion
  192.7 5.5 copy.62
  198.3 4.4 fusion
  204.6 11.7 %cholesky.222 = f32[128,128]{1,0:T(8,128)S(1)} custom-call(f32[128,128]{1,0:T(8,128)S(1)} %cholesky.577), custom_call_target="Cholesky" | custom-call | tf_op jit(solution)/shard_map/jit(cholesky)/cholesky | solution.py:22
  216.4 9.8 %custom-call.66 = f32[1,128,128]{1,2,0:T(8,128)S(1)} custom-call(f32[1,128,128]{2,1,0:T(8,128)S(1)} %get-tuple-element.64), custom_call_target="InvertDiagBlocksLowerTriangular" | custom-call | tf_op jit(solution)/shard_map/jit(cholesky)/cholesky | solution.py:22
  229.3 11.7 %cholesky.243 = f32[128,128]{1,0:T(8,128)S(1)} custom-call(f32[128,128]{1,0:T(8,128)S(1)} %cholesky.581), custom_call_target="Cholesky" | custom-call | tf_op jit(solution)/shard_map/jit(cholesky)/cholesky | solution.py:22
  241.8 9.8 %custom-call.67 = f32[1,128,128]{1,2,0:T(8,128)S(1)} custom-call(f32[1,128,128]{2,1,0:T(8,128)S(1)} %get-tuple-element.62), custom_call_target="InvertDiagBlocksLowerTriangular" | custom-call | tf_op jit(solution)/shard_map/jit(cholesky)/cholesky | solution.py:22
  254.7 2.4 convolution_subtract_fusion.6
  257.2 11.7 %cholesky.466 = f32[128,128]{1,0:T(8,128)S(1)} custom-call(f32[128,128]{1,0:T(8,128)S(1)} %cholesky.586), custom_call_target="Cholesky" | custom-call | tf_op jit(solution)/shard_map/jit(cholesky)/cholesky | solution.py:22
  269.7 9.8 %custom-call.68 = f32[1,128,128]{1,2,0:T(8,128)S(1)} custom-call(f32[1,128,128]{2,1,0:T(8,128)S(1)} %get-tuple-element.60), custom_call_target="InvertDiagBlocksLowerTriangular" | custom-call | tf_op jit(solution)/shard_map/jit(cholesky)/cholesky | solution.py:22
  280.7 3.3 convolution_subtract_fusion.7
  284.0 11.7 %cholesky.485 = f32[128,128]{1,0:T(8,128)S(1)} custom-call(f32[128,128]{1,0:T(8,128)S(1)} %cholesky.591), custom_call_target="Cholesky" | custom-call | tf_op jit(solution)/shard_map/jit(cholesky)/cholesky | solution.py:22
  296.5 9.8 %custom-call.69 = f32[1,128,128]{1,2,0:T(8,128)S(1)} custom-call(f32[1,128,128]{2,1,0:T(8,128)S(1)} %get-tuple-element.58), custom_call_target="InvertDiagBlocksLowerTriangular" | custom-call | tf_op jit(solution)/shard_map/jit(cholesky)/cholesky | solution.py:22
  307.4 3.2 convolution_subtract_fusion.8
  310.6 12.1 %cholesky.504 = f32[128,128]{1,0:T(8,128)S(1)} custom-call(f32[128,128]{1,0:T(8,128)S(1)} %cholesky.596), custom_call_target="Cholesky" | custom-call | tf_op jit(solution)/shard_map/jit(cholesky)/cholesky | solution.py:22
  323.5 9.8 %custom-call.70 = f32[1,128,128]{1,2,0:T(8,128)S(1)} custom-call(f32[1,128,128]{2,1,0:T(8,128)S(1)} %get-tuple-element.56), custom_call_target="InvertDiagBlocksLowerTriangular" | custom-call | tf_op jit(solution)/shard_map/jit(cholesky)/cholesky | solution.py:22
  334.4 3.2 convolution_subtract_fusion.9
  337.7 11.7 %cholesky.524 = f32[128,128]{1,0:T(8,128)S(1)} custom-call(f32[128,128]{1,0:T(8,128)S(1)} %cholesky.601), custom_call_target="Cholesky" | custom-call | tf_op jit(solution)/shard_map/jit(cholesky)/cholesky | solution.py:22
  350.2 9.8 %custom-call.71 = f32[1,128,128]{1,2,0:T(8,128)S(1)} custom-call(f32[1,128,128]{2,1,0:T(8,128)S(1)} %get-tuple-element.54), custom_call_target="InvertDiagBlocksLowerTriangular" | custom-call | tf_op jit(solution)/shard_map/jit(cholesky)/cholesky | solution.py:22
  361.0 2.9 convolution_subtract_fusion.10
  363.9 11.7 %cholesky.544 = f32[128,128]{1,0:T(8,128)S(1)} custom-call(f32[128,128]{1,0:T(8,128)S(1)} %cholesky.606), custom_call_target="Cholesky" | custom-call | tf_op jit(solution)/shard_map/jit(cholesky)/cholesky | solution.py:22
  376.3 9.8 %custom-call.72 = f32[1,128,128]{1,2,0:T(8,128)S(1)} custom-call(f32[1,128,128]{2,1,0:T(8,128)S(1)} %get-tuple-element.52), custom_call_target="InvertDiagBlocksLowerTriangular" | custom-call | tf_op jit(solution)/shard_map/jit(cholesky)/cholesky | solution.py:22
  389.3 11.7 %cholesky.562 = f32[128,128]{1,0:T(8,128)S(1)} custom-call(f32[128,128]{1,0:T(8,128)S(1)} %convolution_subtract_fusion.11), custom_call_target="Cholesky" | custom-call | tf_op jit(solution)/shard_map/jit(cholesky)/cholesky | solution.py:22
  411.4 4.8 select_select_fusion
  416.2 28.3 %while.1 = (s32[]{:T(128)}, f32[1024,1024]{0,1:T(8,128)}, s32[8,2]{0,1:T(2,128)S(1)}, f32[8,128,128]{2,1,0:T(8,128)}, s32[]{:T(128)}) while((s32[]{:T(128)}, f32[1024,1024]{0,1:T(8,128)}, s32[8,2]{0,1:T(2,128)S(1)}, f32[8,128,128]{2,1,0:T(8,128)}, s32[]{:T(128)}) %tuple.57), condition=%wide.while_cond, body=%wide.while_body.sunk | while | flops 2 | bytes 393829 | solution.py:36
  444.5 79.8 %custom-call.73 = f32[8,128,128]{1,2,0:T(8,128)S(1)} custom-call(f32[8,128,128]{2,1,0:T(8,128)} %get-tuple-element.9), custom_call_target="InvertDiagBlocksLowerTriangular" | custom-call | tf_op jit(solution)/shard_map/jit(_solve_triangular)/triangular_solve | solution.py:36
  537.5 2.7 convolution_subtract_fusion.2
  540.9 2.9 convolution_subtract_fusion.1
  544.5 3.4 convolution_subtract_fusion.3
  548.6 4.3 collective-permute-done
  552.9 5.0 fusion.50
  557.9 5.0 reshape.131
  562.9 141.7 %all-reduce.8.cloned.1.call-done = f32[32,32768]{1,0:T(8,128)} async-done(((f32[32,32768]{1,0:T(8,128)}), f32[32,32768]{1,0:T(8,128)}) %all-reduce.8.cloned.1.call-update) | async-done | bytes 4194320
  706.7 62.5 %all-gather.3.cloned.1.call-done = bf16[32,1,32768]{2,1,0:T(2,128)(2,1)} async-done(((bf16[1,1,32768]{2,1,0:T(2,128)(2,1)}), bf16[32,1,32768]{2,1,0:T(2,128)(2,1)}) %all-gather.3.cloned.1.call-update) | async-done | bytes 2097168 | tf_op jit(solution)/shard_map/all_gather | solution.py:73
  769.2 12.5 %reduce.50 = bf16[32,32768]{1,0:T(8,128)(2,1)S(1)} reduce(bf16[32,1,32768]{2,1,0:T(2,128)(2,1)} %all-gather.3.cloned.1.call-done, bf16[]{:T(256)} %constant.330), dimensions={1}, to_apply=%all-gather.reduce_sub_computation | reduce | bytes 4194306 | tf_op jit(solution)/shard_map/all_gather | solution.py:73
  784.1 4.1 copy.79
  788.2 10.1 %fusion.1 = f32[1024,1024]{1,0:T(8,128)} fusion(bf16[1024,1024]{0,1:T(8,128)(2,1)} %collective-permute-done, bf16[1024,1024]{0,1:T(8,128)(2,1)} %copy.79, bf16[1024,1024]{1,0:T(8,128)(2,1)S(1)} %copy-done.4, pred[]{:T(512)S(6)} %eq.7, bf16[1024,1024]{1,0:T(8,128)(2,1)} %copy-done.5), kind=kOutput, calls=%fused_computation.13 | convolution fusion | flops 4300210176 | bytes 12582913 | tf_op jit(solution)/shard_map/dot_general | solution.py:33
  809.9 3.0 fusion.11
  817.6 2.9 fusion.83
  820.5 2.5 constant_dynamic-update-slice_fusion.28
  828.0 3.9 fusion.78
  831.9 2.5 constant_dynamic-update-slice_fusion.35
  840.4 4.5 fusion.72
  853.2 9.5 %multiply_reduce_fusion = f32[]{:T(128)} fusion(bf16[32,1,32768]{2,1,0:T(2,128)(2,1)S(1)} %copy-done.1), kind=kLoop, calls=%fused_computation.5 | loop fusion | flops 3145727 | bytes 2097156 | tf_op jit(solution)/shard_map/reduce_sum | solution.py:75
  (184 shorter events, 110.3 us)
Async XLA Ops:
  7.2 179.9 %all-reduce.6.cloned.1.call-start = ((), (), s32[]{:S(2)}) async-start(), calls=%async_computation | async-start | bytes 8388608 | tf_op jit(solution)/shard_map/psum | solution.py:50
  14.6 690.1 %all-reduce.8.cloned.1.call-start = ((), (), s32[]{:S(2)}) async-start(), calls=%async_computation.2 | async-start | bytes 8388608
  202.7 1.9 copy-start.3
  252.8 2.0 copy-start
  524.4 291.3 %copy-start.6 = (f32[8,128,128]{1,2,0:T(8,128)}, f32[8,128,128]{1,2,0:T(8,128)S(1)}, u32[]{:S(2)}) copy-start(f32[8,128,128]{1,2,0:T(8,128)S(1)} %custom-call.73) | copy-start | bytes 1572868
  524.4 4.5 copy-start.2
  548.5 9.4 %copy-start.5 = (bf16[1024,1024]{1,0:T(8,128)(2,1)}, bf16[1024,1024]{1,0:T(8,128)(2,1)S(1)}, u32[]{:S(2)}) copy-start(bf16[1024,1024]{1,0:T(8,128)(2,1)S(1)} %fusion.41) | copy-start | bytes 6291460
  548.5 4.4 collective-permute-start
  562.9 206.3 %all-gather.3.cloned.1.call-start = ((), (), s32[]{:S(2)}) async-start(), calls=%async_computation.1 | async-start | bytes 4325376 | tf_op jit(solution)/shard_map/all_gather | solution.py:73
  784.1 4.1 copy-start.4
  840.3 10.6 %copy-start.10 = (bf16[128,1024]{0,1:T(8,128)(2,1)S(1)}, bf16[128,1024]{0,1:T(8,128)(2,1)}, u32[]{:S(2)}) copy-start(bf16[128,1024]{0,1:T(8,128)(2,1)} %copy.84) | copy-start | bytes 786436
  840.3 10.7 %copy-start.9 = (bf16[128,1024]{0,1:T(8,128)(2,1)S(1)}, bf16[128,1024]{0,1:T(8,128)(2,1)}, u32[]{:S(2)}) copy-start(bf16[128,1024]{0,1:T(8,128)(2,1)} %copy.85) | copy-start | bytes 786436
  840.3 10.8 %copy-start.8 = (bf16[128,1024]{0,1:T(8,128)(2,1)S(1)}, bf16[128,1024]{0,1:T(8,128)(2,1)}, u32[]{:S(2)}) copy-start(bf16[128,1024]{0,1:T(8,128)(2,1)} %copy.86) | copy-start | bytes 786436
  840.3 10.9 %copy-start.7 = (bf16[128,1024]{0,1:T(8,128)(2,1)S(1)}, bf16[128,1024]{0,1:T(8,128)(2,1)}, u32[]{:S(2)}) copy-start(bf16[128,1024]{0,1:T(8,128)(2,1)} %copy.87) | copy-start | bytes 786436
  849.8 3.5 copy-start.1
Sparse Core Ops, SparseCore 0:
  14.7 172.2 all-reduce.5
  563.0 141.6 all-reduce.7
  708.2 60.9 all-gather.2
where the time goes:
time: 877 us; the launch traced here: 871 us
  waiting for transfers between devices  329 us (38%)
  other arithmetic  289 us (33%)
  matrix products  106 us (12%)
  local copies, waits for them, and re-layouts  77.1 us (9%)
  blocking collectives  47.7 us (5%)
  between operations  23 us (3%)
    another operation x30, other arithmetic, whitening(): factor_lower = jnp.linalg.cholesky(covariance)  168 us
    unnamed x4, waiting for transfers between devices  142 us
    psum x1, waiting for transfers between devices, on_device(): lax.psum((gram_part, column_part, count_part), ('depth', 'sub'))  120 us
    another operation x3, other arithmetic, gradient_rows(): jax.scipy.linalg.solve_triangular(factor_lower, back_rows.T, lower=True,...  84.6 us
    all_gather x1, waiting for transfers between devices, on_device(): lax.all_gather(share_bf, ('tower', 'depth', 'sub'), axis=0, tiled=True)  62.5 us
    psum x1, blocking collectives, on_device(): lax.psum((gram_part, column_part, count_part), ('depth', 'sub'))  47.7 us
    another operation x15, matrix products, gradient_rows(): jax.scipy.linalg.solve_triangular(factor_lower, back_rows.T, lower=True,...  34.7 us
    another operation x40, local copies, waits for them, and re-layouts  28.2 us
  transfers between devices with their start and end apart: 4, of which 4 were waited for; matrix products, arithmetic and copies ran while one was open for 0% of the time, Pallas kernels for 0%

commit v1 on v0

--- a/solution.py
+++ b/solution.py
@@ -70,7 +70,19 @@
         tiled=True,
     )
     share_bf = (cross_share / (count_total - 1.0)).astype(jnp.bfloat16)
-    gathered = lax.all_gather(share_bf, ("tower", "depth", "sub"), axis=0, tiled=True)
+    local_next = lax.axis_size(("tower", "depth", "sub"))
+    item_now = lax.axis_index(("tower", "depth", "sub"))
+    z_new, part_now = (local_next, item_now)
+    gathered, heard = (share_bf, 1)
+    while heard < z_new:
+        column = []
+        for b in range(z_new):
+            column.append((b, b ^ heard))
+        far_arr = lax.ppermute(gathered, axis_name=("tower", "depth", "sub"), perm=column)
+        finding = jnp.concatenate([gathered, far_arr], 0)
+        arr_now = jnp.concatenate([far_arr, gathered], 0)
+        gathered = jnp.where(part_now & heard == 0, finding, arr_now)
+        heard = 2 * heard
     cross_bf = gathered.reshape(feature_width, feature_width)
     corr_mean = jnp.sum(jnp.square(cross_bf.astype(jnp.float32))) / feature_width
     turned = jnp.where(log_tower, cross_bf, cross_bf.T)

time: 877 us -> 832 us (0.949)
  waiting for transfers between devices: 329 us -> 301 us
  other arithmetic: 289 us -> 270 us
    all_gather x1 -> x0, waiting for transfers between devices: 62.5 us -> none  [on_device(): lax.all_gather(share_bf, ('tower', 'depth', 'sub'), axis=0, tiled=True)]
    ppermute x0 -> x5, waiting for transfers between devices: none -> 35.2 us  [on_device(): lax.ppermute(gathered, axis_name=('tower', 'depth', 'sub'), perm=column)]
    all_gather x1 -> x0, other arithmetic: 12.5 us -> none  [on_device(): lax.all_gather(share_bf, ('tower', 'depth', 'sub'), axis=0, tiled=True)]
    unnamed x4 -> x3, waiting for transfers between devices: 142 us -> 142 us
  transfers between devices with their start and end apart: 4 -> 8, of which waited for: 4 -> 8; matrix products, arithmetic and copies ran while one was open for 0% -> 0% of each run, Pallas kernels for 0% -> 0%
where the time goes in v1:
time: 832 us; the launch traced here: 826 us
  waiting for transfers between devices  301 us (36%)
  other arithmetic  270 us (32%)
  matrix products  106 us (13%)
  local copies, waits for them, and re-layouts  72.7 us (9%)
  blocking collectives  47.7 us (6%)
  between operations  23.2 us (3%)
    another operation x30, other arithmetic, whitening(): factor_lower = jnp.linalg.cholesky(covariance)  167 us
    unnamed x3, waiting for transfers between devices  142 us
    psum x1, waiting for transfers between devices, on_device(): lax.psum((gram_part, column_part, count_part), ('depth', 'sub'))  120 us
    another operation x3, other arithmetic, gradient_rows(): jax.scipy.linalg.solve_triangular(factor_lower, back_rows.T, lower=True,...  83.6 us
    psum x1, blocking collectives, on_device(): lax.psum((gram_part, column_part, count_part), ('depth', 'sub'))  47.7 us
    ppermute x5, waiting for transfers between devices, on_device(): lax.ppermute(gathered, axis_name=('tower', 'depth', 'sub'), perm=column)  35.2 us
    another operation x15, matrix products, gradient_rows(): jax.scipy.linalg.solve_triangular(factor_lower, back_rows.T, lower=True,...  34.7 us
    another operation x14, matrix products, whitening(): factor_lower = jnp.linalg.cholesky(covariance)  26.6 us
  transfers between devices with their start and end apart: 8, of which 8 were waited for; matrix products, arithmetic and copies ran while one was open for 0% of the time, Pallas kernels for 0%

profile of v1, /device:TPU:0, one launch (start us, length us, event | category | flops | bytes accessed | tf_op | source)
XLA Modules:
  0.0 826.2 jit_solution(9911768373295503937)
XLA Ops:
  7.9 6.7 fusion.19
  14.6 2.9 copy.33
  18.0 47.7 %all-reduce.2 = (f32[1024]{0:T(1024)S(1)}, f32[]{:T(128)}) all-reduce(f32[1024]{0:T(1024)S(1)} %convert_reduce_fusion, f32[]{:T(128)} %bitcast.3), channel_id=1, replica_groups=mesh['tower'=2,'depth'=4,'sub'=4] {'depth','sub'}, use_global_device_ids=true, to_apply=%region_2.3 | all-reduce | flops 1025 | bytes 8200 | tf_op jit(solution)/shard_map/psum | solution.py:50
  67.0 120.1 %all-reduce.6.cloned.1.call-done = f32[1024,1024]{0,1:T(8,128)} async-done(((f32[1024,1024]{0,1:T(8,128)}), f32[1024,1024]{0,1:T(8,128)}) %all-reduce.6.cloned.1.call-update) | async-done | bytes 4194320 | tf_op jit(solution)/shard_map/psum | solution.py:50
  187.1 5.7 select_add_fusion
  192.8 5.5 copy.34
  198.3 4.4 fusion
  204.7 11.7 %cholesky.222 = f32[128,128]{1,0:T(8,128)S(1)} custom-call(f32[128,128]{1,0:T(8,128)S(1)} %cholesky.577), custom_call_target="Cholesky" | custom-call | tf_op jit(solution)/shard_map/jit(cholesky)/cholesky | solution.py:22
  216.4 9.8 %custom-call.66 = f32[1,128,128]{1,2,0:T(8,128)S(1)} custom-call(f32[1,128,128]{2,1,0:T(8,128)S(1)} %get-tuple-element.62), custom_call_target="InvertDiagBlocksLowerTriangular" | custom-call | tf_op jit(solution)/shard_map/jit(cholesky)/cholesky | solution.py:22
  229.3 11.7 %cholesky.243 = f32[128,128]{1,0:T(8,128)S(1)} custom-call(f32[128,128]{1,0:T(8,128)S(1)} %cholesky.581), custom_call_target="Cholesky" | custom-call | tf_op jit(solution)/shard_map/jit(cholesky)/cholesky | solution.py:22
  241.7 9.8 %custom-call.67 = f32[1,128,128]{1,2,0:T(8,128)S(1)} custom-call(f32[1,128,128]{2,1,0:T(8,128)S(1)} %get-tuple-element.60), custom_call_target="InvertDiagBlocksLowerTriangular" | custom-call | tf_op jit(solution)/shard_map/jit(cholesky)/cholesky | solution.py:22
  257.0 11.7 %cholesky.466 = f32[128,128]{1,0:T(8,128)S(1)} custom-call(f32[128,128]{1,0:T(8,128)S(1)} %cholesky.586), custom_call_target="Cholesky" | custom-call | tf_op jit(solution)/shard_map/jit(cholesky)/cholesky | solution.py:22
  269.5 9.8 %custom-call.68 = f32[1,128,128]{1,2,0:T(8,128)S(1)} custom-call(f32[1,128,128]{2,1,0:T(8,128)S(1)} %get-tuple-element.58), custom_call_target="InvertDiagBlocksLowerTriangular" | custom-call | tf_op jit(solution)/shard_map/jit(cholesky)/cholesky | solution.py:22
  280.5 3.5 convolution_subtract_fusion.7
  284.1 11.7 %cholesky.485 = f32[128,128]{1,0:T(8,128)S(1)} custom-call(f32[128,128]{1,0:T(8,128)S(1)} %cholesky.591), custom_call_target="Cholesky" | custom-call | tf_op jit(solution)/shard_map/jit(cholesky)/cholesky | solution.py:22
  296.6 9.8 %custom-call.69 = f32[1,128,128]{1,2,0:T(8,128)S(1)} custom-call(f32[1,128,128]{2,1,0:T(8,128)S(1)} %get-tuple-element.56), custom_call_target="InvertDiagBlocksLowerTriangular" | custom-call | tf_op jit(solution)/shard_map/jit(cholesky)/cholesky | solution.py:22
  307.5 3.2 convolution_subtract_fusion.8
  310.7 11.9 %cholesky.504 = f32[128,128]{1,0:T(8,128)S(1)} custom-call(f32[128,128]{1,0:T(8,128)S(1)} %cholesky.596), custom_call_target="Cholesky" | custom-call | tf_op jit(solution)/shard_map/jit(cholesky)/cholesky | solution.py:22
  323.3 9.8 %custom-call.70 = f32[1,128,128]{1,2,0:T(8,128)S(1)} custom-call(f32[1,128,128]{2,1,0:T(8,128)S(1)} %get-tuple-element.54), custom_call_target="InvertDiagBlocksLowerTriangular" | custom-call | tf_op jit(solution)/shard_map/jit(cholesky)/cholesky | solution.py:22
  334.3 3.2 convolution_subtract_fusion.9
  337.5 11.7 %cholesky.524 = f32[128,128]{1,0:T(8,128)S(1)} custom-call(f32[128,128]{1,0:T(8,128)S(1)} %cholesky.601), custom_call_target="Cholesky" | custom-call | tf_op jit(solution)/shard_map/jit(cholesky)/cholesky | solution.py:22
  350.0 9.8 %custom-call.71 = f32[1,128,128]{1,2,0:T(8,128)S(1)} custom-call(f32[1,128,128]{2,1,0:T(8,128)S(1)} %get-tuple-element.52), custom_call_target="InvertDiagBlocksLowerTriangular" | custom-call | tf_op jit(solution)/shard_map/jit(cholesky)/cholesky | solution.py:22
  360.8 3.1 convolution_subtract_fusion.10
  363.9 11.7 %cholesky.544 = f32[128,128]{1,0:T(8,128)S(1)} custom-call(f32[128,128]{1,0:T(8,128)S(1)} %cholesky.606), custom_call_target="Cholesky" | custom-call | tf_op jit(solution)/shard_map/jit(cholesky)/cholesky | solution.py:22
  376.4 9.8 %custom-call.72 = f32[1,128,128]{1,2,0:T(8,128)S(1)} custom-call(f32[1,128,128]{2,1,0:T(8,128)S(1)} %get-tuple-element.50), custom_call_target="InvertDiagBlocksLowerTriangular" | custom-call | tf_op jit(solution)/shard_map/jit(cholesky)/cholesky | solution.py:22
  389.4 11.7 %cholesky.562 = f32[128,128]{1,0:T(8,128)S(1)} custom-call(f32[128,128]{1,0:T(8,128)S(1)} %convolution_subtract_fusion.11), custom_call_target="Cholesky" | custom-call | tf_op jit(solution)/shard_map/jit(cholesky)/cholesky | solution.py:22
  411.5 4.8 select_select_fusion
  416.4 24.1 %while.1 = (s32[]{:T(128)}, f32[1024,1024]{0,1:T(8,128)}, s32[8,2]{0,1:T(2,128)S(1)}, f32[8,128,128]{2,1,0:T(8,128)S(1)}, s32[]{:T(128)}) while((s32[]{:T(128)}, f32[1024,1024]{0,1:T(8,128)}, s32[8,2]{0,1:T(2,128)S(1)}, f32[8,128,128]{2,1,0:T(8,128)S(1)}, s32[]{:T(128)}) %tuple.57), condition=%wide.while_cond, body=%wide.while_body.sunk | while | flops 2 | bytes 393321 | solution.py:36
  440.5 78.8 %custom-call.73 = f32[8,128,128]{1,2,0:T(8,128)S(1)} custom-call(f32[8,128,128]{2,1,0:T(8,128)S(1)} %get-tuple-element.9), custom_call_target="InvertDiagBlocksLowerTriangular" | custom-call | tf_op jit(solution)/shard_map/jit(_solve_triangular)/triangular_solve | solution.py:36
  532.4 2.7 convolution_subtract_fusion.2
  535.8 2.9 convolution_subtract_fusion.1
  539.3 3.5 convolution_subtract_fusion.3
  543.6 4.3 collective-permute-done
  547.8 5.0 fusion.50
  552.8 5.0 reshape.133
  557.8 141.6 %all-reduce.8.cloned.1.call-done = f32[32,32768]{1,0:T(8,128)} async-done(((f32[32,32768]{1,0:T(8,128)}), f32[32,32768]{1,0:T(8,128)}) %all-reduce.8.cloned.1.call-update) | async-done | bytes 4194320
  702.3 3.6 collective-permute-done.1
  707.9 3.6 collective-permute-done.2
  712.8 7.5 collective-permute-done.3
  721.9 17.7 %collective-permute-done.4 = bf16[8,32768]{1,0:T(8,128)(2,1)S(1)} collective-permute-done((bf16[8,32768]{1,0:T(8,128)(2,1)S(1)}, bf16[8,32768]{1,0:T(8,128)(2,1)S(1)}, u32[]{:S(2)}, u32[]{:S(2)}) %collective-permute-start.4) | collective-permute-done | bytes 524320 | tf_op jit(solution)/shard_map/ppermute | solution.py:81
  739.9 2.8 collective-permute-done.5
  742.6 2.9 multiply_reduce_fusion
  747.9 4.5 copy.51
  752.4 10.2 %fusion.1 = f32[1024,1024]{1,0:T(8,128)} fusion(bf16[1024,1024]{0,1:T(8,128)(2,1)} %collective-permute-done, bf16[1024,1024]{0,1:T(8,128)(2,1)} %copy.51, bf16[1024,1024]{1,0:T(8,128)(2,1)S(1)} %copy-done.3, pred[]{:T(512)S(6)} %eq.22, bf16[1024,1024]{1,0:T(8,128)(2,1)} %copy-done.4), kind=kOutput, calls=%fused_computation.13 | convolution fusion | flops 4300210176 | bytes 12582913 | tf_op jit(solution)/shard_map/dot_general | solution.py:33
  774.1 3.0 fusion.11
  781.8 2.8 fusion.83
  792.3 3.8 fusion.78
  804.7 4.5 fusion.72
  (194 shorter events, 119.0 us)
Async XLA Ops:
  7.2 179.9 %all-reduce.6.cloned.1.call-start = ((), (), s32[]{:S(2)}) async-start(), calls=%async_computation | async-start | bytes 8388608 | tf_op jit(solution)/shard_map/psum | solution.py:50
  14.6 684.9 %all-reduce.8.cloned.1.call-start = ((), (), s32[]{:S(2)}) async-start(), calls=%async_computation.1 | async-start | bytes 8388608
  202.7 1.9 copy-start.2
  252.6 2.0 copy-start
  519.3 23.6 %copy-start.5 = (f32[8,128,128]{1,2,0:T(8,128)}, f32[8,128,128]{1,2,0:T(8,128)S(1)}, u32[]{:S(2)}) copy-start(f32[8,128,128]{1,2,0:T(8,128)S(1)} %custom-call.73) | copy-start | bytes 1572868
  519.3 4.5 copy-start.1
  543.5 9.4 %copy-start.4 = (bf16[1024,1024]{1,0:T(8,128)(2,1)}, bf16[1024,1024]{1,0:T(8,128)(2,1)S(1)}, u32[]{:S(2)}) copy-start(bf16[1024,1024]{1,0:T(8,128)(2,1)S(1)} %fusion.41) | copy-start | bytes 6291460
  543.5 4.4 collective-permute-start
  700.9 5.0 collective-permute-start.1
  706.5 5.0 collective-permute-start.2
  712.0 8.4 %collective-permute-start.3 = (bf16[4,32768]{1,0:T(4,128)(2,1)S(1)}, bf16[4,32768]{1,0:T(4,128)(2,1)S(1)}, u32[]{:S(2)}, u32[]{:S(2)}) collective-permute-start(bf16[4,32768]{1,0:T(4,128)(2,1)S(1)} %maximum_select_fusion.3), channel_id=1, source_target_pairs={{0,4},{1,5},{2,6},{3,7},{4,0},{5,1},{6,2},{7,3},{8,12},{9,13},{10,... | collective-permute-start | bytes 786440 | tf_op jit(solution)/shard_map/ppermute | solution.py:81
  720.8 18.8 %collective-permute-start.4 = (bf16[8,32768]{1,0:T(8,128)(2,1)S(1)}, bf16[8,32768]{1,0:T(8,128)(2,1)S(1)}, u32[]{:S(2)}, u32[]{:S(2)}) collective-permute-start(bf16[8,32768]{1,0:T(8,128)(2,1)S(1)} %maximum_select_fusion.2), channel_id=1, source_target_pairs={{0,8},{1,9},{2,10},{3,11},{4,12},{5,13},{6,14},{7,15},{8,0},{9,1},... | collective-permute-start | bytes 1572872 | tf_op jit(solution)/shard_map/ppermute | solution.py:81
  739.8 2.9 collective-permute-start.5
  747.9 4.5 copy-start.3
  752.3 10.2 %copy-start.6 = (f32[8,128,128]{1,2,0:T(8,128)S(1)}, f32[8,128,128]{1,2,0:T(8,128)}, u32[]{:S(2)}) copy-start(f32[8,128,128]{1,2,0:T(8,128)} %copy-done.5) | copy-start | bytes 1572868
  804.6 10.5 %copy-start.10 = (bf16[128,1024]{0,1:T(8,128)(2,1)S(1)}, bf16[128,1024]{0,1:T(8,128)(2,1)}, u32[]{:S(2)}) copy-start(bf16[128,1024]{0,1:T(8,128)(2,1)} %copy.55) | copy-start | bytes 786436
  804.7 10.6 %copy-start.9 = (bf16[128,1024]{0,1:T(8,128)(2,1)S(1)}, bf16[128,1024]{0,1:T(8,128)(2,1)}, u32[]{:S(2)}) copy-start(bf16[128,1024]{0,1:T(8,128)(2,1)} %copy.56) | copy-start | bytes 786436
  804.7 10.7 %copy-start.8 = (bf16[128,1024]{0,1:T(8,128)(2,1)S(1)}, bf16[128,1024]{0,1:T(8,128)(2,1)}, u32[]{:S(2)}) copy-start(bf16[128,1024]{0,1:T(8,128)(2,1)} %copy.57) | copy-start | bytes 786436
  804.7 10.8 %copy-start.7 = (bf16[128,1024]{0,1:T(8,128)(2,1)S(1)}, bf16[128,1024]{0,1:T(8,128)(2,1)}, u32[]{:S(2)}) copy-start(bf16[128,1024]{0,1:T(8,128)(2,1)} %copy.58) | copy-start | bytes 786436
Sparse Core Ops, SparseCore 0:
  14.7 172.3 all-reduce.5
  558.0 141.4 all-reduce.7
